TPU v7x, 512 devices: a whole 4x4x16 slice. The times are simulated.
512 devices in a mesh: wide: 128 (over z, y, core), pair: 4 (over x).
Axes of the slice: x: 4, y: 4, z: 16, core: 2. Of those that a mesh axis runs over, the one named last changes fastest.
Arguments:
- three_center: bfloat16 [512, 8, 1024], P('wide'), may hold values from -0.3125 to 0.3125
- occ_green: bfloat16 [512, 128, 8, 8], P('wide', 'pair'), may hold values from -2 to 2
- virt_green: bfloat16 [512, 128, 8, 8], P('wide', 'pair'), may hold values from -2 to 2
- occ_column: int32 [512, 128], P('wide', 'pair'), may hold values from 0 to 511, as said below
- partner_live: int32 [512, 128], P('wide', 'pair'), may hold values 0 or 1
Outputs:
- response: float32 [128, 128], P('pair')
Inputs may be any that keep to these rules, and one draw needn't show every extreme that they name: `occ_column`: for each index of pair and each index w of wide, the slots of that group on the 4 atom blocks w * 4 to w * 4 + 3 name partner blocks k such that no value of k // 4 occurs more than 2 times, and some value occurs exactly 2 times.
All inputs are finite; a program needn't handle non-finite values. No bound on the sum of `partner_live` on one device may be relied on, other than what follows from the above.
Results may differ from a plain program's by a relative error of at most 0.004.
Values may be sent and summed in bfloat16 or wider, within the bound.
A program may use at most 64 MiB of HBM per device.

v0:
```python
import jax
import jax.numpy as jnp
from jax import lax
from jax.sharding import PartitionSpec as P

CAP = 2


def apply_virtual(occupied, virt_blocks, block_size):
    shaped = occupied.reshape(occupied.shape[:-1] + (block_size, -1))
    product = jnp.einsum(
        "...lnp,...ns->...lsp", shaped, virt_blocks, preferred_element_type=jnp.float32
    )
    return product.astype(jnp.bfloat16).reshape(occupied.shape)


def slot_ranks(owners):
    unit_count = owners.shape[-1]
    same_owner = owners[..., :, None] == owners[..., None, :]
    before = jnp.arange(unit_count)[None, :] < jnp.arange(unit_count)[:, None]
    return jnp.sum(same_owner & before, axis=-1)


def local(three_center, occ_green, virt_green, occ_column, partner_live):
    local_atoms, block_size, wide_row = three_center.shape
    aux_count = wide_row // block_size
    wide_count = lax.axis_size("wide")
    slot_total = wide_count * CAP
    unit_count = occ_green.shape[0] * occ_green.shape[1]
    listed = lax.all_gather(occ_column, "wide", axis=0, tiled=True).reshape(wide_count, unit_count)
    listed_owner = listed // local_atoms
    listed_rank = slot_ranks(listed_owner)
    to_here = listed_owner == lax.axis_index("wide")
    chosen = to_here[:, None, :] & (listed_rank[:, None, :] == jnp.arange(CAP)[None, :, None])
    slot_atom = jnp.sum(jnp.where(chosen, (listed % local_atoms)[:, None, :], 0), axis=2).reshape(
        slot_total
    )
    slot_used = jnp.any(chosen, axis=2).reshape(slot_total)
    occupied = jnp.einsum(
        "amnl,anx->amlx", occ_green, three_center, preferred_element_type=jnp.float32
    )
    occupied = occupied * partner_live.astype(jnp.float32)[:, :, None, None]
    occupied = occupied.astype(jnp.bfloat16).reshape(unit_count, block_size, wide_row)
    owners = (occ_column // local_atoms).reshape(unit_count)
    position = owners * CAP + slot_ranks(owners)
    virt_units = virt_green.reshape(unit_count, block_size, block_size)
    own_rows = three_center.astype(jnp.float32).reshape(-1, aux_count)
    both = apply_virtual(occupied, virt_units, block_size)
    outgoing = jnp.zeros((slot_total, block_size, wide_row), jnp.bfloat16).at[position].set(both)
    arrived = lax.all_to_all(
        outgoing.reshape(wide_count, CAP, block_size, wide_row),
        "wide",
        split_axis=0,
        concat_axis=0,
        tiled=True,
    )
    routing = (
        (slot_atom[None, :] == jnp.arange(local_atoms)[:, None]) & slot_used[None, :]
    ).astype(jnp.bfloat16)
    partner_sum = jnp.dot(
        routing, arrived.reshape(slot_total, -1), preferred_element_type=jnp.float32
    )
    partner_rows = partner_sum.reshape(-1, aux_count)
    response_part = lax.dot_general(
        partner_rows,
        own_rows,
        (((0,), (0,)), ((), ())),
        precision=lax.Precision.HIGHEST,
        preferred_element_type=jnp.float32,
    )
    total = lax.psum(response_part, ("wide", "pair"))
    row_count = aux_count // lax.axis_size("pair")
    result = lax.dynamic_slice_in_dim(total, lax.axis_index("pair") * row_count, row_count, 0)
    return result


def solution(mesh):
    placed = (
        P("wide", None, None),
        P("wide", "pair", None, None),
        P("wide", "pair", None, None),
        P("wide", "pair"),
        P("wide", "pair"),
    )
    return jax.shard_map(
        local, mesh=mesh, in_specs=placed, out_specs=P("pair", None), check_vma=False
    )
```

profile of v0, /device:TPU:1, one launch (start us, length us, event | category | flops | bytes accessed | tf_op | source)
XLA Modules:
  0.0 793.3 jit_solution(15315771442357756404)
XLA Ops:
  6.5 0.7 broadcast_multiply_fusion
  7.2 0.1 mul.26
  7.3 0.1 eq.80
  7.4 0.2 convert_reduce_fusion.1
  7.6 1.1 copy.39
  8.7 1.1 copy.33
  9.8 0.7 convert_element_type.22
  10.5 1.5 multiply_convert_fusion
  12.0 2.0 convert_bitcast_fusion
  14.1 2.8 reshape.166
  16.9 2.5 broadcast_in_dim.12
  19.4 15.7 %scatter_fusion = bf16[256,8,1024]{2,1,0:T(8,128)(2,1)} fusion(bf16[256,8,1024]{2,1,0:T(8,128)(2,1)} %broadcast_in_dim.12, s32[128]{0:T(128)S(1)} %fusion.17, bf16[128,8,1024]{2,1,0:T(8,128)(2,1)S(1)} %reshape.166), kind=kCustom, calls=%fused_computation | custom fusion | bytes 6291968 | tf_op jit(solution)/shard_map/scatter | solution.py:49
  35.1 0.0 copy-start
  35.1 0.0 copy-start.1
  35.1 21.1 %all-to-all-start = ((bf16[128,2,8,1024]{3,2,1,0:T(8,128)(2,1)}), bf16[128,2,8,1024]{3,2,1,0:T(8,128)(2,1)}, u32[]{:S(2)}, u32[]{:S(2)}) async-start(bf16[128,2,8,1024]{3,2,1,0:T(8,128)(2,1)} %bitcast.58), calls=%async_computation | async-start | bytes 8388608 | tf_op jit(solution)/shard_map/all_to_all | solution.py:50
  56.3 0.0 all-reduce.2.cloned.1.call-start
  56.3 0.0 copy-done
  56.4 0.0 copy-done.1
  56.4 276.5 %all-gather = s32[128,4,32]{2,1,0:T(4,128)S(1)} all-gather(s32[1,4,32]{2,1,0:T(4,128)S(1)} %bitcast.62), channel_id=1, replica_groups=mesh['wide'=128,'pair'=4] {'wide'}, dimensions={0}, use_global_device_ids=true | all-gather | bytes 66048 | tf_op jit(solution)/shard_map/all_gather | solution.py:30
  332.9 0.1 copy.26
  333.1 0.1 copy.30
  333.2 0.1 broadcast_compare_fusion
  333.2 0.1 copy.28
  333.3 0.1 copy.27
  333.5 5.1 convert_reduce_fusion
  338.6 0.1 select_reduce_fusion
  338.7 0.1 copy.31
  338.8 0.1 eq.76
  339.0 0.1 fusion.5
  339.1 0.1 copy.32
  339.2 0.2 and.81
  339.4 0.0 all-to-all-done
  339.4 6.5 copy.41
  345.9 0.7 fusion.11
  346.6 0.1 reshape.160
  346.7 0.9 fusion.18
  347.6 0.0 all-reduce.2.cloned.1.call-update
  347.6 437.5 %all-reduce.2.cloned.1.call-done = f32[128,128]{1,0:T(8,128)} async-done(((f32[128,128]{1,0:T(8,128)}), f32[128,128]{1,0:T(8,128)}) %all-reduce.2.cloned.1.call-update) | async-done | bytes 65552 | tf_op jit(solution)/shard_map/psum | solution.py:71
  785.1 1.3 constant_dynamic-slice_fusion
  (4 shorter events, 0.1 us)
Async XLA Ops:
  35.1 21.2 %copy-start = (bf16[4,8,1024]{2,1,0:T(8,128)(2,1)S(1)}, bf16[4,8,1024]{2,1,0:T(8,128)(2,1)}, u32[]{:S(2)}) copy-start(bf16[4,8,1024]{2,1,0:T(8,128)(2,1)} %param.5) | copy-start | bytes 196612
  35.1 21.3 %copy-start.1 = (s32[4,32]{1,0:T(4,128)S(1)}, s32[4,32]{1,0:T(4,128)}, u32[]{:S(2)}) copy-start(s32[4,32]{1,0:T(4,128)} %param.8) | copy-start | bytes 1540
  35.1 304.2 %all-to-all-start = ((bf16[128,2,8,1024]{3,2,1,0:T(8,128)(2,1)}), bf16[128,2,8,1024]{3,2,1,0:T(8,128)(2,1)}, u32[]{:S(2)}, u32[]{:S(2)}) async-start(bf16[128,2,8,1024]{3,2,1,0:T(8,128)(2,1)} %bitcast.58), calls=%async_computation | async-start | bytes 8388608 | tf_op jit(solution)/shard_map/all_to_all | solution.py:50
  56.3 728.9 %all-reduce.2.cloned.1.call-start = ((), (), s32[]{:S(2)}) async-start(), calls=%async_computation.1 | async-start | bytes 131072 | tf_op jit(solution)/shard_map/psum | solution.py:71
Sparse Core Ops, SparseCore 0:
  347.7 437.3 all-reduce.1
where the time goes:
time: 794 us; the launch traced here: 793 us
  waiting for transfers between devices  438 us (55%)
  blocking collectives  277 us (35%)
  local copies, waits for them, and re-layouts  32.4 us (4%)
  starting transfers between devices  21.2 us (3%)
  between operations  13.6 us (2%)
    psum x1, waiting for transfers between devices, local(): total = lax.psum(response_part, ('wide', 'pair'))  438 us
    all_gather x1, blocking collectives, local(): lax.all_gather(occ_column, 'wide', axis=0, tiled=True)  277 us
    all_to_all x1, starting transfers between devices, local(): lax.all_to_all(outgoing.reshape(wide_count, CAP, block_size, wide_row), '...  21.1 us
  transfers between devices with their start and end apart: 2, of which 1 were waited for; matrix products, arithmetic and copies ran while one was open for 1% of the time, Pallas kernels for 0%

commit v1 on v0

--- a/solution.py
+++ b/solution.py
@@ -68,7 +68,9 @@
         precision=lax.Precision.HIGHEST,
         preferred_element_type=jnp.float32,
     )
-    total = lax.psum(response_part, ("wide", "pair"))
+    total = response_part
+    for w in ("wide", "pair"):
+        total = lax.psum(total, axis_name=w)
     row_count = aux_count // lax.axis_size("pair")
     result = lax.dynamic_slice_in_dim(total, lax.axis_index("pair") * row_count, row_count, 0)
     return result

time: 794 us -> 714 us (0.90)
  waiting for transfers between devices: 438 us -> 356 us
    psum x1 -> x2, waiting for transfers between devices: 438 us -> 356 us  [local(): total = lax.psum(total, axis_name=w)]
  transfers between devices with their start and end apart: 2 -> 3, of which waited for: 1 -> 2; matrix products, arithmetic and copies ran while one was open for 1% -> 1% of each run, Pallas kernels for 0% -> 0%
where the time goes in v1:
time: 714 us; the launch traced here: 712 us
  waiting for transfers between devices  356 us (50%)
  blocking collectives  277 us (39%)
  local copies, waits for them, and re-layouts  32.4 us (5%)
  starting transfers between devices  21.2 us (3%)
  between operations  13.6 us (2%)
    psum x2, waiting for transfers between devices, local(): total = lax.psum(total, axis_name=w)  356 us
    all_gather x1, blocking collectives, local(): lax.all_gather(occ_column, 'wide', axis=0, tiled=True)  277 us
    all_to_all x1, starting transfers between devices, local(): lax.all_to_all(outgoing.reshape(wide_count, CAP, block_size, wide_row), '...  21.1 us
    scatter x1, local copies, waits for them, and re-layouts, local(): jnp.zeros((slot_total, block_size, wide_row), jnp.bfloat16).at[position]  15.7 us
  transfers between devices with their start and end apart: 3, of which 2 were waited for; matrix products, arithmetic and copies ran while one was open for 1% of the time, Pallas kernels for 0%

profile of v1, /device:TPU:1, one launch (start us, length us, event | category | flops | bytes accessed | tf_op | source)
XLA Modules:
  0.0 711.9 jit_solution(1897298928600355254)
XLA Ops:
  6.5 0.7 broadcast_multiply_fusion
  7.2 0.1 mul.26
  7.3 0.1 eq.80
  7.4 0.2 convert_reduce_fusion.1
  7.6 1.1 copy.39
  8.7 1.1 copy.33
  9.8 0.7 convert_element_type.22
  10.5 1.5 multiply_convert_fusion
  12.0 2.0 convert_bitcast_fusion
  14.1 2.8 reshape.166
  16.9 2.5 broadcast_in_dim.12
  19.4 15.7 %scatter_fusion = bf16[256,8,1024]{2,1,0:T(8,128)(2,1)} fusion(bf16[256,8,1024]{2,1,0:T(8,128)(2,1)} %broadcast_in_dim.12, s32[128]{0:T(128)S(1)} %fusion.17, bf16[128,8,1024]{2,1,0:T(8,128)(2,1)S(1)} %reshape.166), kind=kCustom, calls=%fused_computation | custom fusion | bytes 6291968 | tf_op jit(solution)/shard_map/scatter | solution.py:49
  35.1 0.0 copy-start
  35.1 0.0 copy-start.1
  35.1 21.1 %all-to-all-start = ((bf16[128,2,8,1024]{3,2,1,0:T(8,128)(2,1)}), bf16[128,2,8,1024]{3,2,1,0:T(8,128)(2,1)}, u32[]{:S(2)}, u32[]{:S(2)}) async-start(bf16[128,2,8,1024]{3,2,1,0:T(8,128)(2,1)} %bitcast.58), calls=%async_computation | async-start | bytes 8388608 | tf_op jit(solution)/shard_map/all_to_all | solution.py:50
  56.3 0.0 all-reduce.3.cloned.1.call-start
  56.3 0.0 copy-done
  56.4 0.0 copy-done.1
  56.4 276.5 %all-gather = s32[128,4,32]{2,1,0:T(4,128)S(1)} all-gather(s32[1,4,32]{2,1,0:T(4,128)S(1)} %bitcast.62), channel_id=1, replica_groups=mesh['wide'=128,'pair'=4] {'wide'}, dimensions={0}, use_global_device_ids=true | all-gather | bytes 66048 | tf_op jit(solution)/shard_map/all_gather | solution.py:30
  332.9 0.1 copy.26
  333.1 0.1 copy.30
  333.2 0.1 broadcast_compare_fusion
  333.2 0.1 copy.28
  333.3 0.1 copy.27
  333.5 5.1 convert_reduce_fusion
  338.6 0.1 select_reduce_fusion
  338.7 0.1 copy.31
  338.8 0.1 eq.76
  339.0 0.1 fusion.5
  339.1 0.1 copy.32
  339.2 0.2 and.81
  339.4 0.0 all-to-all-done
  339.4 6.5 copy.41
  345.9 0.7 fusion.11
  346.6 0.1 reshape.160
  346.7 0.9 fusion.18
  347.6 0.0 all-reduce.3.cloned.1.call-update
  347.6 0.0 all-reduce.5.cloned.1.call-start
  347.6 307.2 %all-reduce.3.cloned.1.call-done = f32[128,128]{1,0:T(8,128)} async-done(((f32[128,128]{1,0:T(8,128)}), f32[128,128]{1,0:T(8,128)}) %all-reduce.3.cloned.1.call-update) | async-done | bytes 65552 | tf_op jit(solution)/shard_map/psum | solution.py:73
  654.8 0.0 all-reduce.5.cloned.1.call-update
  654.9 48.9 %all-reduce.5.cloned.1.call-done = f32[128,128]{1,0:T(8,128)} async-done(((f32[128,128]{1,0:T(8,128)}), f32[128,128]{1,0:T(8,128)}) %all-reduce.5.cloned.1.call-update) | async-done | bytes 65552 | tf_op jit(solution)/shard_map/psum | solution.py:73
  703.7 1.3 constant_dynamic-slice_fusion
  (4 shorter events, 0.1 us)
Async XLA Ops:
  35.1 21.2 %copy-start = (bf16[4,8,1024]{2,1,0:T(8,128)(2,1)S(1)}, bf16[4,8,1024]{2,1,0:T(8,128)(2,1)}, u32[]{:S(2)}) copy-start(bf16[4,8,1024]{2,1,0:T(8,128)(2,1)} %param.5) | copy-start | bytes 196612
  35.1 21.3 %copy-start.1 = (s32[4,32]{1,0:T(4,128)S(1)}, s32[4,32]{1,0:T(4,128)}, u32[]{:S(2)}) copy-start(s32[4,32]{1,0:T(4,128)} %param.8) | copy-start | bytes 1540
  35.1 304.2 %all-to-all-start = ((bf16[128,2,8,1024]{3,2,1,0:T(8,128)(2,1)}), bf16[128,2,8,1024]{3,2,1,0:T(8,128)(2,1)}, u32[]{:S(2)}, u32[]{:S(2)}) async-start(bf16[128,2,8,1024]{3,2,1,0:T(8,128)(2,1)} %bitcast.58), calls=%async_computation | async-start | bytes 8388608 | tf_op jit(solution)/shard_map/all_to_all | solution.py:50
  56.3 598.6 %all-reduce.3.cloned.1.call-start = ((), (), s32[]{:S(2)}) async-start(), calls=%async_computation.1 | async-start | bytes 131072 | tf_op jit(solution)/shard_map/psum | solution.py:73
  347.6 356.1 %all-reduce.5.cloned.1.call-start = ((), (), s32[]{:S(2)}) async-start(), calls=%async_computation.2 | async-start | bytes 131072 | tf_op jit(solution)/shard_map/psum | solution.py:73
Sparse Core Ops, SparseCore 0:
  347.7 307.0 all-reduce.2
  657.1 46.5 all-reduce.4

commit v2 on v0

--- a/solution.py
+++ b/solution.py
@@ -1,9 +1,18 @@
+import functools
 import jax
 import jax.numpy as jnp
 from jax import lax
 from jax.sharding import PartitionSpec as P
 
 CAP = 2
+
+
+def find_values_here(panel, across):
+    long_array = lax.all_to_all(jnp.stack(lax.axis_size(across) * [panel], axis=0), across, 0, 0)
+    return jnp.concatenate(long_array, axis=0)
+
+
+derive_tails_now = functools.partial(find_values_here, across="wide")
 
 
 def apply_virtual(occupied, virt_blocks, block_size):
@@ -27,7 +36,7 @@
     wide_count = lax.axis_size("wide")
     slot_total = wide_count * CAP
     unit_count = occ_green.shape[0] * occ_green.shape[1]
-    listed = lax.all_gather(occ_column, "wide", axis=0, tiled=True).reshape(wide_count, unit_count)
+    listed = derive_tails_now(occ_column).reshape(wide_count, unit_count)
     listed_owner = listed // local_atoms
     listed_rank = slot_ranks(listed_owner)
     to_here = listed_owner == lax.axis_index("wide")

time: 794 us -> 713 us (0.90)
  blocking collectives: 277 us -> 0 us
  waiting for transfers between devices: 438 us -> 613 us
  starting transfers between devices: 21.2 us -> 37.5 us
    all_gather x1 -> x0, blocking collectives: 277 us -> none  [local(): lax.all_gather(occ_column, 'wide', axis=0, tiled=True)]
    all_to_all x1, waiting for transfers between devices: 0.01 us -> 175 us  [local(): lax.all_to_all(outgoing.reshape(wide_count, CAP, block_size, wide_row), '...]
    all_to_all x0 -> x1, starting transfers between devices: none -> 20.6 us  [find_values_here(): lax.all_to_all(jnp.stack(lax.axis_size(across) * [panel], axis=0), across...]
  transfers between devices with their start and end apart: 2 -> 3, of which waited for: 1 -> 2; matrix products, arithmetic and copies ran while one was open for 1% -> 5% of each run, Pallas kernels for 0% -> 0%
where the time goes in v2:
time: 713 us; the launch traced here: 712 us
  waiting for transfers between devices  613 us (86%)
  starting transfers between devices  37.5 us (5%)
  local copies, waits for them, and re-layouts  34.6 us (5%)
  between operations  13.6 us (2%)
  other arithmetic  7.81 us (1%)
    psum x1, waiting for transfers between devices, local(): total = lax.psum(response_part, ('wide', 'pair'))  438 us
    all_to_all x1, waiting for transfers between devices, local(): lax.all_to_all(outgoing.reshape(wide_count, CAP, block_size, wide_row), '...  175 us
    all_to_all x1, starting transfers between devices, find_values_here(): lax.all_to_all(jnp.stack(lax.axis_size(across) * [panel], axis=0), across...  20.6 us
    all_to_all x1, starting transfers between devices, local(): lax.all_to_all(outgoing.reshape(wide_count, CAP, block_size, wide_row), '...  16.7 us
    scatter x1, local copies, waits for them, and re-layouts, local(): jnp.zeros((slot_total, block_size, wide_row), jnp.bfloat16).at[position]  15.7 us
  transfers between devices with their start and end apart: 3, of which 2 were waited for; matrix products, arithmetic and copies ran while one was open for 5% of the time, Pallas kernels for 0%

profile of v2, /device:TPU:1, one launch (start us, length us, event | category | flops | bytes accessed | tf_op | source)
XLA Modules:
  0.0 712.0 jit_solution(8486088965007823313)
XLA Ops:
  6.5 0.7 stack.2
  7.3 0.8 reshape.170
  8.1 20.6 %all-to-all-start = ((s32[128,1,128]{2,1,0:T(1,128)}), s32[128,1,128]{2,1,0:T(1,128)S(1)}, u32[]{:S(2)}, u32[]{:S(2)}) async-start(s32[128,1,128]{2,1,0:T(1,128)} %reshape.170), calls=%async_computation | async-start | bytes 131072 | tf_op jit(solution)/shard_map/all_to_all | solution.py:11
  28.6 0.7 broadcast_multiply_fusion
  29.3 0.1 eq.80
  29.4 1.1 copy.38
  30.5 1.1 copy.32
  31.6 0.7 convert_element_type.22
  32.3 1.5 multiply_convert_fusion
  33.9 2.0 convert_bitcast_fusion
  35.9 0.2 convert_reduce_fusion.1
  36.1 0.1 mul.26
  36.2 2.8 reshape.164
  39.0 2.5 broadcast_in_dim.12
  41.5 15.7 %scatter_fusion = bf16[256,8,1024]{2,1,0:T(8,128)(2,1)} fusion(bf16[256,8,1024]{2,1,0:T(8,128)(2,1)} %broadcast_in_dim.12, s32[128]{0:T(128)S(1)} %fusion.17, bf16[128,8,1024]{2,1,0:T(8,128)(2,1)S(1)} %reshape.164), kind=kCustom, calls=%fused_computation | custom fusion | bytes 6291968 | tf_op jit(solution)/shard_map/scatter | solution.py:58
  57.2 0.0 all-to-all-done
  57.2 0.0 copy-start
  57.2 16.7 %all-to-all-start.1 = ((bf16[128,2,8,1024]{3,2,1,0:T(8,128)(2,1)}), bf16[128,2,8,1024]{3,2,1,0:T(8,128)(2,1)}, u32[]{:S(2)}, u32[]{:S(2)}) async-start(bf16[128,2,8,1024]{3,2,1,0:T(8,128)(2,1)} %bitcast.57), calls=%async_computation.1 | async-start | bytes 8388608 | tf_op jit(solution)/shard_map/all_to_all | solution.py:59
  73.9 0.2 all-reduce.2.cloned.1.call-start
  74.2 0.0 copy-done
  74.2 0.5 broadcast.149
  74.8 0.8 reduce
  75.6 0.2 reshape.171
  75.7 0.1 copy.25
  75.9 0.1 copy.29
  76.0 0.1 broadcast_compare_fusion
  76.0 0.1 copy.27
  76.1 0.1 copy.26
  76.3 5.1 convert_reduce_fusion
  81.4 0.1 select_reduce_fusion
  81.5 0.1 copy.30
  81.6 0.1 eq.76
  81.8 0.1 fusion.5
  81.9 0.1 copy.31
  82.0 0.2 and.81
  82.2 175.3 %all-to-all-done.1 = bf16[128,2,8,1024]{3,2,1,0:T(8,128)(2,1)} async-done(((bf16[128,2,8,1024]{3,2,1,0:T(8,128)(2,1)}), bf16[128,2,8,1024]{3,2,1,0:T(8,128)(2,1)}, u32[]{:S(2)}, u32[]{:S(2)}) %all-to-all-start.1) | async-done | bytes 4194336 | tf_op jit(solution)/shard_map/all_to_all | solution.py:59
  257.4 6.5 copy.40
  264.0 0.7 fusion.11
  264.6 0.1 reshape.158
  264.7 0.9 fusion.18
  265.6 0.0 all-reduce.2.cloned.1.call-update
  265.7 438.2 %all-reduce.2.cloned.1.call-done = f32[128,128]{1,0:T(8,128)} async-done(((f32[128,128]{1,0:T(8,128)}), f32[128,128]{1,0:T(8,128)}) %all-reduce.2.cloned.1.call-update) | async-done | bytes 65552 | tf_op jit(solution)/shard_map/psum | solution.py:80
  703.8 1.3 constant_dynamic-slice_fusion
  (4 shorter events, 0.1 us)
Async XLA Ops:
  8.1 49.2 %all-to-all-start = ((s32[128,1,128]{2,1,0:T(1,128)}), s32[128,1,128]{2,1,0:T(1,128)S(1)}, u32[]{:S(2)}, u32[]{:S(2)}) async-start(s32[128,1,128]{2,1,0:T(1,128)} %reshape.170), calls=%async_computation | async-start | bytes 131072 | tf_op jit(solution)/shard_map/all_to_all | solution.py:11
  57.2 16.9 %copy-start = (bf16[4,8,1024]{2,1,0:T(8,128)(2,1)S(1)}, bf16[4,8,1024]{2,1,0:T(8,128)(2,1)}, u32[]{:S(2)}) copy-start(bf16[4,8,1024]{2,1,0:T(8,128)(2,1)} %param.5) | copy-start | bytes 196612
  57.2 200.2 %all-to-all-start.1 = ((bf16[128,2,8,1024]{3,2,1,0:T(8,128)(2,1)}), bf16[128,2,8,1024]{3,2,1,0:T(8,128)(2,1)}, u32[]{:S(2)}, u32[]{:S(2)}) async-start(bf16[128,2,8,1024]{3,2,1,0:T(8,128)(2,1)} %bitcast.57), calls=%async_computation.1 | async-start | bytes 8388608 | tf_op jit(solution)/shard_map/all_to_all | solution.py:59
  73.9 629.9 %all-reduce.2.cloned.1.call-start = ((), (), s32[]{:S(2)}) async-start(), calls=%async_computation.2 | async-start | bytes 131072 | tf_op jit(solution)/shard_map/psum | solution.py:80
Sparse Core Ops, SparseCore 0:
  265.8 438.0 all-reduce.1

commit v3 on v0

--- a/solution.py
+++ b/solution.py
@@ -68,7 +68,8 @@
         precision=lax.Precision.HIGHEST,
         preferred_element_type=jnp.float32,
     )
-    total = lax.psum(response_part, ("wide", "pair"))
+    parts = lax.all_gather(response_part, ("wide", "pair"), axis=0, tiled=False)
+    total = parts.sum(axis=0)
     row_count = aux_count // lax.axis_size("pair")
     result = lax.dynamic_slice_in_dim(total, lax.axis_index("pair") * row_count, row_count, 0)
     return result

time: 794 us -> 605 us (0.76)
  waiting for transfers between devices: 438 us -> 236 us
  other arithmetic: 7.01 us -> 20.1 us
    psum x1 -> x0, waiting for transfers between devices: 438 us -> none  [local(): total = lax.psum(response_part, ('wide', 'pair'))]
    all_gather x0 -> x1, waiting for transfers between devices: none -> 236 us  [local(): parts = lax.all_gather(response_part, ('wide', 'pair'), axis=0, tiled=False)]
    reduce_sum x0 -> x1, other arithmetic: none -> 13.1 us  [local(): total = parts.sum(axis=0)]
where the time goes in v3:
time: 605 us; the launch traced here: 604 us
  blocking collectives  276 us (46%)
  waiting for transfers between devices  236 us (39%)
  local copies, waits for them, and re-layouts  31.6 us (5%)
  starting transfers between devices  21.2 us (4%)
  other arithmetic  20.1 us (3%)
  between operations  13.6 us (2%)
    all_gather x1, blocking collectives, local(): lax.all_gather(occ_column, 'wide', axis=0, tiled=True)  276 us
    all_gather x1, waiting for transfers between devices, local(): parts = lax.all_gather(response_part, ('wide', 'pair'), axis=0, tiled=False)  236 us
    all_to_all x1, starting transfers between devices, local(): lax.all_to_all(outgoing.reshape(wide_count, CAP, block_size, wide_row), '...  21.1 us
    scatter x1, local copies, waits for them, and re-layouts, local(): jnp.zeros((slot_total, block_size, wide_row), jnp.bfloat16).at[position]  15.7 us
    reduce_sum x1, other arithmetic, local(): total = parts.sum(axis=0)  13.1 us
  transfers between devices with their start and end apart: 2, of which 1 were waited for; matrix products, arithmetic and copies ran while one was open for 1% of the time, Pallas kernels for 0%

profile of v3, /device:TPU:1, one launch (start us, length us, event | category | flops | bytes accessed | tf_op | source)
XLA Modules:
  0.0 603.8 jit_solution(11082680124360632235)
XLA Ops:
  6.5 0.7 convert_element_type.22
  7.2 0.7 broadcast_multiply_fusion
  7.9 0.1 mul.26
  8.0 0.1 eq.80
  8.1 0.2 convert_reduce_fusion.1
  8.3 1.1 copy.33
  9.4 1.1 copy.39
  10.5 1.5 multiply_convert_fusion
  12.0 2.0 convert_bitcast_fusion
  14.1 2.8 reshape.166
  16.9 2.5 broadcast_in_dim.12
  19.4 15.7 %scatter_fusion = bf16[256,8,1024]{2,1,0:T(8,128)(2,1)} fusion(bf16[256,8,1024]{2,1,0:T(8,128)(2,1)} %broadcast_in_dim.12, s32[128]{0:T(128)S(1)} %fusion.17, bf16[128,8,1024]{2,1,0:T(8,128)(2,1)S(1)} %reshape.166), kind=kCustom, calls=%fused_computation | custom fusion | bytes 6291968 | tf_op jit(solution)/shard_map/scatter | solution.py:49
  35.1 0.0 copy-start
  35.1 0.0 copy-start.1
  35.1 21.1 %all-to-all-start = ((bf16[128,2,8,1024]{3,2,1,0:T(8,128)(2,1)}), bf16[128,2,8,1024]{3,2,1,0:T(8,128)(2,1)}, u32[]{:S(2)}, u32[]{:S(2)}) async-start(bf16[128,2,8,1024]{3,2,1,0:T(8,128)(2,1)} %bitcast.61), calls=%async_computation | async-start | bytes 8388608 | tf_op jit(solution)/shard_map/all_to_all | solution.py:50
  56.3 0.0 all-gather.4.cloned.1.call-start
  56.3 0.0 copy-done
  56.4 0.0 copy-done.1
  56.4 276.5 %all-gather.1 = s32[128,4,32]{2,1,0:T(4,128)S(1)} all-gather(s32[1,4,32]{2,1,0:T(4,128)S(1)} %bitcast.65), channel_id=1, replica_groups=mesh['wide'=128,'pair'=4] {'wide'}, dimensions={0}, use_global_device_ids=true | all-gather | bytes 66048 | tf_op jit(solution)/shard_map/all_gather | solution.py:30
  332.9 0.1 copy.26
  333.1 0.1 copy.30
  333.2 0.1 broadcast_compare_fusion
  333.2 0.1 copy.27
  333.3 0.1 copy.28
  333.5 5.1 convert_reduce_fusion
  338.6 0.1 fusion.5
  338.7 0.1 copy.32
  338.8 0.2 and.81
  339.0 0.1 select_reduce_fusion
  339.1 0.1 copy.31
  339.2 0.1 eq.76
  339.4 0.0 all-to-all-done
  339.4 6.5 %copy.41 = bf16[32,8,8,1024]{3,1,2,0:T(8,128)(2,1)S(1)} copy(bf16[32,8,8,1024]{3,2,1,0:T(8,128)(2,1)} %bitcast.18) | data formatting | bytes 8388608
  345.9 0.7 fusion.11
  346.6 0.1 reshape.160
  346.7 0.9 fusion.18
  347.6 0.0 all-gather.4.cloned.1.call-update
  347.6 235.7 %all-gather.4.cloned.1.call-done = f32[65536,128]{1,0:T(8,128)} async-done(((f32[128,128]{1,0:T(8,128)}), f32[65536,128]{1,0:T(8,128)}) %all-gather.4.cloned.1.call-update) | async-done | bytes 33554448 | tf_op jit(solution)/shard_map/all_gather | solution.py:71
  583.3 13.1 %reduce_sum.42 = f32[128,128]{1,0:T(8,128)S(1)} reduce(f32[512,128,128]{2,1,0:T(8,128)} %bitcast.60, f32[]{:T(128)} %constant.57.clone.1), dimensions={0}, to_apply=%region_5.6 | reduce | flops 8372224 | bytes 33619972 | tf_op jit(solution)/shard_map/reduce_sum | solution.py:72
  596.4 0.6 constant_dynamic-slice_fusion
  (4 shorter events, 0.1 us)
Async XLA Ops:
  35.1 21.2 %copy-start = (bf16[4,8,1024]{2,1,0:T(8,128)(2,1)S(1)}, bf16[4,8,1024]{2,1,0:T(8,128)(2,1)}, u32[]{:S(2)}) copy-start(bf16[4,8,1024]{2,1,0:T(8,128)(2,1)} %param.5) | copy-start | bytes 196612
  35.1 21.3 %copy-start.1 = (s32[4,32]{1,0:T(4,128)S(1)}, s32[4,32]{1,0:T(4,128)}, u32[]{:S(2)}) copy-start(s32[4,32]{1,0:T(4,128)} %param.8) | copy-start | bytes 1540
  35.1 304.2 %all-to-all-start = ((bf16[128,2,8,1024]{3,2,1,0:T(8,128)(2,1)}), bf16[128,2,8,1024]{3,2,1,0:T(8,128)(2,1)}, u32[]{:S(2)}, u32[]{:S(2)}) async-start(bf16[128,2,8,1024]{3,2,1,0:T(8,128)(2,1)} %bitcast.61), calls=%async_computation | async-start | bytes 8388608 | tf_op jit(solution)/shard_map/all_to_all | solution.py:50
  56.3 527.0 %all-gather.4.cloned.1.call-start = ((), (), s32[]{:S(2)}) async-start(), calls=%async_computation.1 | async-start | bytes 33619968 | tf_op jit(solution)/shard_map/all_gather | solution.py:71
Sparse Core Ops, SparseCore 0:
  347.7 235.5 all-gather.3
